TPU v7x, 32 devices: a whole 2x2x4 slice. The times are simulated.
32 devices in a mesh: domain: 8 (over y, x, core), band: 4 (over z).
Axes of the slice: x: 2, y: 2, z: 4, core: 2. Of those that a mesh axis runs over, the one named last changes fastest.
Arguments:
- psi: float32 [4, 48, 32, 128], P('band', 'domain'), may hold values from -6 to 6
- potential: float32 [48, 32, 128], P('domain', 'band'), may hold values from -2 to 2
- projectors: float32 [8, 8, 2, 8, 1024], P('domain'), may hold values from -0.1875 to 0.1875
- offsets: int32 [8, 8, 2], P('domain'), may hold values from 0 to 184
- intersection: int32 [8, 8, 2], P('domain'), may hold values from -1 to 31, as said below
- dmat: float32 [256, 8, 8], P('domain'), may hold values from -9 to 9
Outputs:
- filtered: float32 [4, 48, 32, 128], P('band', 'domain')
Inputs may be any that keep to these rules, and one draw needn't show every extreme that they name: intersection[s, d, k] is -1 for an empty slot, else the index among the 32 atoms owned by domain device d of an atom whose projector reaches into domain device s's block; in every draw some owner d receives all 2 slots live from every source s. `offsets`: footprints are whole runs of 8 tiles inside the source block and may intersection one another.
All inputs are finite; a program needn't handle non-finite values.
Results may differ from a plain program's by a relative error of at most 0.00022.
Values sent between devices are 32-bit elements; how exact they have to be, the bound alone decides.
No kernel may reach another device: no remote copies, remote signals or barrier semaphores. Data moves between devices by JAX's collectives and lax.ppermute only.
A program may use at most 64 MiB of HBM per device.

v0:
```python
import jax
import jax.numpy as jnp
from jax import lax
from jax.sharding import PartitionSpec as P

DEGREE = 4
stencil_weights = (
    -5369.0 / 1800.0,
    12.0 / 7.0,
    -15.0 / 56.0,
    10.0 / 189.0,
    -1.0 / 112.0,
    2.0 / 1925.0,
    -1.0 / 16632.0,
)
filter_center = 6.0
filter_half_width = 4.0
highest = lax.Precision.HIGHEST


def extended(value, sides, width):
    for axis, dim in sides:
        size, length = (lax.axis_size(axis), value.shape[dim])
        up = [(i, (i + 1) % size) for i in range(size - 1)]
        down = [(j, i) for i, j in up]
        last = lax.slice_in_dim(value, length - width, length, axis=dim)
        initial = lax.slice_in_dim(value, 0, width, axis=dim)
        before = lax.ppermute(last, axis, up)
        after = lax.ppermute(initial, axis, down)
        value = jnp.concatenate([before, value, after], axis=dim)
    return value


def kinetic(grid_field, padded, reach_cells):
    planes = grid_field.shape[0]
    summed = 3.0 * stencil_weights[0] * grid_field
    for distance in range(1, reach_cells + 1):
        beside_all = (
            padded[reach_cells + distance : reach_cells + distance + planes]
            + padded[reach_cells - distance : reach_cells - distance + planes]
        )
        beside_all = (
            beside_all + jnp.roll(grid_field, distance, 1) + jnp.roll(grid_field, -distance, 1)
        )
        beside_all = (
            beside_all + jnp.roll(grid_field, distance, 2) + jnp.roll(grid_field, -distance, 2)
        )
        summed = summed + stencil_weights[distance] * beside_all
    return -0.5 * summed


def shards(psi, potential, projectors, offsets, intersection, dmat):
    reach_cells = len(stencil_weights) - 1
    pot_full = lax.all_gather(potential, "band", axis=1, tiled=True)
    projector_block = projectors[0]
    domains = projector_block.shape[0]
    cap_slots = projector_block.shape[1]
    proj_count = projector_block.shape[2]
    foot_tiles = projector_block.shape[3] // 128
    tile_index = (offsets[0][..., None] + jnp.arange(foot_tiles, dtype=jnp.int32)).reshape(-1)
    slot_atoms = intersection[0]
    live_slots = (slot_atoms >= 0).astype(jnp.float32)
    atom_count = dmat.shape[0]
    incoming = lax.all_to_all(slot_atoms, "domain", split_axis=0, concat_axis=0, tiled=True)
    in_hot = (incoming.reshape(-1)[:, None] == jnp.arange(atom_count, dtype=jnp.int32)).astype(
        jnp.float32
    )

    def owner_side(partial_value):
        received = lax.all_to_all(partial_value, "domain", split_axis=0, concat_axis=0, tiled=True)
        coefficient = jnp.dot(in_hot.T, received.reshape(-1, proj_count), precision=highest)
        applied = jnp.einsum("aij,aj->ai", dmat, coefficient, precision=highest)
        returned = jnp.dot(in_hot, applied, precision=highest).reshape(
            domains, cap_slots, proj_count
        )
        return lax.all_to_all(returned, "domain", split_axis=0, concat_axis=0, tiled=True)

    def hamiltonian(grid_field):
        padded = extended(grid_field, (("domain", 0),), reach_cells)
        tiles = grid_field.reshape(-1, 128)
        footprint = tiles[tile_index].reshape(domains, cap_slots, -1)
        partial_value = (
            jnp.einsum("dkil,dkl->dki", projector_block, footprint, precision=highest)
            * live_slots[..., None]
        )
        returned = owner_side(partial_value)
        contrib = jnp.einsum("dkil,dki->dkl", projector_block, returned, precision=highest).reshape(
            -1, 128
        )
        nonlocal_term = jnp.zeros_like(tiles).at[tile_index].add(contrib).reshape(grid_field.shape)
        return kinetic(grid_field, padded, reach_cells) + pot_full * grid_field + nonlocal_term

    state = psi[0]
    previous = state
    current = (hamiltonian(state) - filter_center * state) / filter_half_width
    for degree in range(1, DEGREE):
        following = (
            2.0 * (hamiltonian(current) - filter_center * current) / filter_half_width - previous
        )
        previous, current = (current, following)
    return current[None]


def solution(mesh):
    return jax.shard_map(
        shards,
        mesh=mesh,
        in_specs=(
            P("band", "domain", None, None),
            P("domain", "band", None),
            P("domain", None, None, None, None),
            P("domain", None, None),
            P("domain", None, None),
            P("domain", None, None),
        ),
        out_specs=P("band", "domain", None, None),
        check_vma=False,
    )
```

profile of v0, /device:TPU:0, one launch (start us, length us, event | category | flops | bytes accessed | tf_op | source)
XLA Modules:
  0.0 173.2 jit_solution(14876016404611144924)
XLA Ops:
  0.0 3.1 %collective-permute-start.1 = (f32[6,32,128]{2,1,0:T(8,128)}, f32[6,32,128]{2,1,0:T(8,128)}, u32[]{:S(2)}, u32[]{:S(2)}) collective-permute-start(f32[6,32,128]{2,1,0:T(8,128)} %bitcast.104), channel_id=1, source_target_pairs={{0,4},{4,8},{8,12},{12,16},{16,20},{20,24},{24,28},{1,5},{5,9},{9,... | collective-permute-start | bytes 294920 | tf_op jit(solution)/shard_map/ppermute | solution.py:28
  3.1 1.3 collective-permute-start
  4.4 1.3 copy.22
  5.8 6.5 %all-to-all-start = ((s32[8,1,2]{2,1,0:T(1,128)}), s32[8,1,2]{2,1,0:T(1,128)S(1)}, u32[]{:S(2)}, u32[]{:S(2)}) async-start(s32[8,1,2]{2,1,0:T(1,128)} %copy.22), calls=%async_computation | async-start | bytes 8192 | tf_op jit(solution)/shard_map/all_to_all | solution.py:64
  12.9 1.4 fusion.327
  14.3 1.4 fusion.331
  15.6 1.4 fusion.335
  19.0 0.7 fusion.326
  19.8 0.7 fusion.325
  21.9 0.7 fusion.345
  25.1 1.1 fusion.14
  26.8 4.2 %all-to-all-start.1 = ((f32[8,2,8]{2,1,0:T(2,128)}), f32[8,2,8]{2,1,0:T(2,128)S(1)}, u32[]{:S(2)}, u32[]{:S(2)}) async-start(f32[8,2,8]{2,1,0:T(2,128)} %broadcast_multiply_fusion.4), calls=%async_computation.1 | async-start | bytes 16384 | tf_op jit(solution)/shard_map/all_to_all | solution.py:70
  32.8 2.9 %all-to-all-done.1 = f32[8,2,8]{2,1,0:T(2,128)S(1)} async-done(((f32[8,2,8]{2,1,0:T(2,128)}), f32[8,2,8]{2,1,0:T(2,128)S(1)}, u32[]{:S(2)}, u32[]{:S(2)}) %all-to-all-start.1) | async-done | bytes 544 | tf_op jit(solution)/shard_map/all_to_all | solution.py:70
  36.5 0.8 fusion.238
  37.3 3.3 %all-to-all-start.2 = ((f32[8,2,8]{2,1,0:T(2,128)}), f32[8,2,8]{2,1,0:T(2,128)S(1)}, u32[]{:S(2)}, u32[]{:S(2)}) async-start(f32[8,2,8]{2,1,0:T(2,128)} %bitcast.15), calls=%async_computation.2 | async-start | bytes 16384 | tf_op jit(solution)/shard_map/all_to_all | solution.py:76
  40.6 13.5 %all_gather.3 = f32[6,32,128]{2,1,0:T(8,128)S(1)} all-gather(f32[6,8,128]{2,1,0:T(8,128)S(1)} %copy-done.18), channel_id=1, replica_groups=mesh['domain'=8,'band'=4] {'band'}, dimensions={1}, use_global_device_ids=true | all-gather | bytes 122880 | tf_op jit(solution)/shard_map/all_gather | solution.py:54
  54.8 1.0 scatter_custom_fusion
  56.7 2.1 %broadcast_multiply_fusion = (f32[6,32,128]{2,1,0:T(8,128)S(1)}, f32[6,32,128]{2,1,0:T(8,128)S(1)}) fusion(f32[6,32,128]{2,1,0:T(8,128)S(1)} %bitcast.131, f32[6,32,128]{2,1,0:T(8,128)S(1)} %bitcast.135, f32[6,32,128]{2,1,0:T(8,128)S(1)} %all_gather.3, f32[6,32,6]{2,1,0:T(8,128)} %get-tuple-element.196, f32[6,32,122]{2,1,0:T(8,128)} %get-tuple-element.198, ...), kind=kLoop, calls=%fused_computation.315 | loop fusion | flops 2064384 | bytes 3047424 | tf_op jit(solution)/shard_map/div | solution.py:95
  61.3 1.9 %collective-permute-start.3 = (f32[6,32,128]{2,1,0:T(8,128)S(1)}, f32[6,32,128]{2,1,0:T(8,128)}, u32[]{:S(2)}, u32[]{:S(2)}) collective-permute-start(f32[6,32,128]{2,1,0:T(8,128)S(1)} %get-tuple-element.5), channel_id=1, source_target_pairs={{0,4},{4,8},{8,12},{12,16},{16,20},{20,24},{24,28},{1,5},{5,9},{9,... | collective-permute-start | bytes 294920 | tf_op jit(solution)/shard_map/ppermute | solution.py:28
  63.2 1.3 collective-permute-start.2
  65.3 0.7 fusion.318
  66.0 0.7 fusion.317
  66.8 0.7 fusion.302
  67.5 0.7 fusion.301
  69.6 0.8 gather_fusion.1
  70.4 1.1 fusion.10
  72.1 6.5 %all-to-all-start.3 = ((f32[8,2,8]{2,1,0:T(2,128)}), f32[8,2,8]{2,1,0:T(2,128)S(1)}, u32[]{:S(2)}, u32[]{:S(2)}) async-start(f32[8,2,8]{2,1,0:T(2,128)} %broadcast_multiply_fusion.3), calls=%async_computation.3 | async-start | bytes 16384 | tf_op jit(solution)/shard_map/all_to_all | solution.py:70
  79.2 4.1 %all-to-all-done.3 = f32[8,2,8]{2,1,0:T(2,128)S(1)} async-done(((f32[8,2,8]{2,1,0:T(2,128)}), f32[8,2,8]{2,1,0:T(2,128)S(1)}, u32[]{:S(2)}, u32[]{:S(2)}) %all-to-all-start.3) | async-done | bytes 544 | tf_op jit(solution)/shard_map/all_to_all | solution.py:70
  83.6 0.8 fusion.236
  84.4 3.3 %all-to-all-start.4 = ((f32[8,2,8]{2,1,0:T(2,128)}), f32[8,2,8]{2,1,0:T(2,128)S(1)}, u32[]{:S(2)}, u32[]{:S(2)}) async-start(f32[8,2,8]{2,1,0:T(2,128)} %bitcast.25), calls=%async_computation.4 | async-start | bytes 16384 | tf_op jit(solution)/shard_map/all_to_all | solution.py:76
  88.3 4.0 %all-to-all-done.4 = f32[8,2,8]{2,1,0:T(2,128)S(1)} async-done(((f32[8,2,8]{2,1,0:T(2,128)}), f32[8,2,8]{2,1,0:T(2,128)S(1)}, u32[]{:S(2)}, u32[]{:S(2)}) %all-to-all-start.4) | async-done | bytes 544 | tf_op jit(solution)/shard_map/all_to_all | solution.py:76
  93.0 1.2 scatter_custom_fusion.1
  95.0 2.1 %multiply_subtract_fusion.1 = f32[6,32,128]{2,1,0:T(8,128)S(1)} fusion(f32[6,32,128]{2,1,0:T(8,128)S(1)} %get-tuple-element.6, f32[6,32,128]{2,1,0:T(8,128)S(1)} %bitcast.136, f32[6,32,128]{2,1,0:T(8,128)S(1)} %all_gather.3, f32[6,32,128]{2,1,0:T(8,128)S(1)} %get-tuple-element.5, f32[6,32,6]{2,1,0:T(8,128)S(1)} %get-tuple-element.148, ...), kind=kLoop, calls=%fused_computation.310 | loop fusion | flops 2088960 | bytes 3145728 | tf_op jit(solution)/shard_map/sub | solution.py:98
  99.5 2.3 %collective-permute-start.5 = (f32[6,32,128]{2,1,0:T(8,128)S(1)}, f32[6,32,128]{2,1,0:T(8,128)}, u32[]{:S(2)}, u32[]{:S(2)}) collective-permute-start(f32[6,32,128]{2,1,0:T(8,128)S(1)} %multiply_subtract_fusion.1), channel_id=1, source_target_pairs={{0,4},{4,8},{8,12},{12,16},{16,20},{20,24},{24,28},{1,5},{5,9},{9,... | collective-permute-start | bytes 294920 | tf_op jit(solution)/shard_map/ppermute | solution.py:28
  101.9 1.3 collective-permute-start.4
  104.0 0.7 fusion.294
  104.7 0.7 fusion.293
  105.5 0.7 fusion.278
  106.2 0.7 fusion.277
  108.3 0.8 gather_fusion.2
  109.1 1.1 fusion.6
  110.8 4.7 %all-to-all-start.5 = ((f32[8,2,8]{2,1,0:T(2,128)}), f32[8,2,8]{2,1,0:T(2,128)S(1)}, u32[]{:S(2)}, u32[]{:S(2)}) async-start(f32[8,2,8]{2,1,0:T(2,128)} %broadcast_multiply_fusion.2), calls=%async_computation.5 | async-start | bytes 16384 | tf_op jit(solution)/shard_map/all_to_all | solution.py:70
  116.1 4.1 %all-to-all-done.5 = f32[8,2,8]{2,1,0:T(2,128)S(1)} async-done(((f32[8,2,8]{2,1,0:T(2,128)}), f32[8,2,8]{2,1,0:T(2,128)S(1)}, u32[]{:S(2)}, u32[]{:S(2)}) %all-to-all-start.5) | async-done | bytes 544 | tf_op jit(solution)/shard_map/all_to_all | solution.py:70
  120.4 0.8 fusion.234
  121.2 3.3 %all-to-all-start.6 = ((f32[8,2,8]{2,1,0:T(2,128)}), f32[8,2,8]{2,1,0:T(2,128)S(1)}, u32[]{:S(2)}, u32[]{:S(2)}) async-start(f32[8,2,8]{2,1,0:T(2,128)} %bitcast.35), calls=%async_computation.6 | async-start | bytes 16384 | tf_op jit(solution)/shard_map/all_to_all | solution.py:76
  125.2 4.0 %all-to-all-done.6 = f32[8,2,8]{2,1,0:T(2,128)S(1)} async-done(((f32[8,2,8]{2,1,0:T(2,128)}), f32[8,2,8]{2,1,0:T(2,128)S(1)}, u32[]{:S(2)}, u32[]{:S(2)}) %all-to-all-start.6) | async-done | bytes 544 | tf_op jit(solution)/shard_map/all_to_all | solution.py:76
  129.9 1.3 scatter_custom_fusion.2
  132.0 2.1 %multiply_subtract_fusion = f32[6,32,128]{2,1,0:T(8,128)S(1)} fusion(f32[6,32,128]{2,1,0:T(8,128)S(1)} %multiply_subtract_fusion.1, f32[6,32,128]{2,1,0:T(8,128)S(1)} %bitcast.137, f32[6,32,128]{2,1,0:T(8,128)S(1)} %all_gather.3, f32[6,32,6]{2,1,0:T(8,128)S(1)} %get-tuple-element.100, f32[6,32,122]{2,1,0:T(8,128)S(1)} %get-tuple-element.102, ...), kind=kLoop, calls=%fused_computation.309 | loop fusion | flops 2113536 | bytes 3047424 | tf_op jit(solution)/shard_map/sub | solution.py:98
  136.6 2.3 %collective-permute-start.7 = (f32[6,32,128]{2,1,0:T(8,128)S(1)}, f32[6,32,128]{2,1,0:T(8,128)}, u32[]{:S(2)}, u32[]{:S(2)}) collective-permute-start(f32[6,32,128]{2,1,0:T(8,128)S(1)} %multiply_subtract_fusion), channel_id=1, source_target_pairs={{0,4},{4,8},{8,12},{12,16},{16,20},{20,24},{24,28},{1,5},{5,9},{9,... | collective-permute-start | bytes 294920 | tf_op jit(solution)/shard_map/ppermute | solution.py:28
  138.9 1.3 collective-permute-start.6
  141.0 0.7 fusion.254
  141.8 0.7 fusion.253
  142.5 0.7 fusion.273
  143.9 0.7 fusion.274
  144.7 0.8 gather_fusion.3
  145.4 1.1 fusion.2
  147.2 4.7 %all-to-all-start.7 = ((f32[8,2,8]{2,1,0:T(2,128)}), f32[8,2,8]{2,1,0:T(2,128)S(1)}, u32[]{:S(2)}, u32[]{:S(2)}) async-start(f32[8,2,8]{2,1,0:T(2,128)} %broadcast_multiply_fusion.1), calls=%async_computation.7 | async-start | bytes 16384 | tf_op jit(solution)/shard_map/all_to_all | solution.py:70
  152.4 4.1 %all-to-all-done.7 = f32[8,2,8]{2,1,0:T(2,128)S(1)} async-done(((f32[8,2,8]{2,1,0:T(2,128)}), f32[8,2,8]{2,1,0:T(2,128)S(1)}, u32[]{:S(2)}, u32[]{:S(2)}) %all-to-all-start.7) | async-done | bytes 544 | tf_op jit(solution)/shard_map/all_to_all | solution.py:70
  156.8 0.8 fusion.232
  157.6 3.3 %all-to-all-start.8 = ((f32[8,2,8]{2,1,0:T(2,128)}), f32[8,2,8]{2,1,0:T(2,128)S(1)}, u32[]{:S(2)}, u32[]{:S(2)}) async-start(f32[8,2,8]{2,1,0:T(2,128)} %bitcast.45), calls=%async_computation.8 | async-start | bytes 16384 | tf_op jit(solution)/shard_map/all_to_all | solution.py:76
  160.9 4.6 %all-to-all-done.8 = f32[8,2,8]{2,1,0:T(2,128)S(1)} async-done(((f32[8,2,8]{2,1,0:T(2,128)}), f32[8,2,8]{2,1,0:T(2,128)S(1)}, u32[]{:S(2)}, u32[]{:S(2)}) %all-to-all-start.8) | async-done | bytes 544 | tf_op jit(solution)/shard_map/all_to_all | solution.py:76
  166.8 1.5 reshape.199
  168.3 1.3 scatter_custom_fusion.3
  170.4 2.7 %subtract_bitcast_fusion = f32[1,6,32,128]{3,2,1,0:T(8,128)} fusion(f32[6,32,128]{2,1,0:T(8,128)S(1)} %multiply_subtract_fusion.1, f32[6,32,128]{2,1,0:T(8,128)S(1)} %multiply_subtract_fusion, f32[6,32,128]{2,1,0:T(8,128)S(1)} %bitcast.134, f32[6,32,128]{2,1,0:T(8,128)S(1)} %all_gather.3, f32[6,32,6]{2,1,0:T(8,128)} %get-tuple-element.52, ...), kind=kLoop, calls=%fused_computation.308 | loop fusion | flops 2088960 | bytes 3047424 | tf_op jit(solution)/shard_map/broadcast_in_dim | solution.py:101
  (180 shorter events, 34.6 us)
Async XLA Ops:
  0.0 25.1 %copy-start = (f32[1,8,2,8,1024]{4,3,2,1,0:T(8,128)S(1)}, f32[1,8,2,8,1024]{4,3,2,1,0:T(8,128)}, u32[]{:S(2)}) copy-start(f32[1,8,2,8,1024]{4,3,2,1,0:T(8,128)} %param.8) | copy-start | bytes 1572868
  0.0 17.0 %copy-start.1 = (f32[1,6,32,128]{3,2,1,0:T(8,128)S(1)}, f32[1,6,32,128]{3,2,1,0:T(8,128)}, u32[]{:S(2)}) copy-start(f32[1,6,32,128]{3,2,1,0:T(8,128)} %param.6) | copy-start | bytes 294916
  0.0 55.9 %collective-permute-start.1 = (f32[6,32,128]{2,1,0:T(8,128)}, f32[6,32,128]{2,1,0:T(8,128)}, u32[]{:S(2)}, u32[]{:S(2)}) collective-permute-start(f32[6,32,128]{2,1,0:T(8,128)} %bitcast.104), channel_id=1, source_target_pairs={{0,4},{4,8},{8,12},{12,16},{16,20},{20,24},{24,28},{1,5},{5,9},{9,... | collective-permute-start | bytes 294920 | tf_op jit(solution)/shard_map/ppermute | solution.py:28
  3.1 52.8 %collective-permute-start = (f32[6,32,128]{2,1,0:T(8,128)}, f32[6,32,128]{2,1,0:T(8,128)}, u32[]{:S(2)}, u32[]{:S(2)}) collective-permute-start(f32[6,32,128]{2,1,0:T(8,128)} %bitcast.105), channel_id=1, source_target_pairs={{4,0},{8,4},{12,8},{16,12},{20,16},{24,20},{28,24},{5,1},{9,5},{13... | collective-permute-start | bytes 294920 | tf_op jit(solution)/shard_map/ppermute | solution.py:29
  5.8 21.1 %all-to-all-start = ((s32[8,1,2]{2,1,0:T(1,128)}), s32[8,1,2]{2,1,0:T(1,128)S(1)}, u32[]{:S(2)}, u32[]{:S(2)}) async-start(s32[8,1,2]{2,1,0:T(1,128)} %copy.22), calls=%async_computation | async-start | bytes 8192 | tf_op jit(solution)/shard_map/all_to_all | solution.py:64
  23.4 0.7 copy-start.23
  24.4 30.5 %copy-start.24 = (s32[128]{0:T(128)}, s32[128]{0:T(128)S(1)}, u32[]{:S(2)}) copy-start(s32[128]{0:T(128)S(1)} %fusion.249) | copy-start | bytes 1540
  24.4 0.7 copy-start.22
  26.8 8.9 %all-to-all-start.1 = ((f32[8,2,8]{2,1,0:T(2,128)}), f32[8,2,8]{2,1,0:T(2,128)S(1)}, u32[]{:S(2)}, u32[]{:S(2)}) async-start(f32[8,2,8]{2,1,0:T(2,128)} %broadcast_multiply_fusion.4), calls=%async_computation.1 | async-start | bytes 16384 | tf_op jit(solution)/shard_map/all_to_all | solution.py:70
  32.8 3.7 %copy-start.25 = (s32[16]{0:T(128)}, s32[16]{0:T(128)S(1)}, u32[]{:S(2)}) copy-start(s32[16]{0:T(128)S(1)} %eq.15) | copy-start | bytes 196
  35.7 0.8 copy-start.2
  36.5 4.1 %copy-start.18 = (f32[6,8,128]{2,1,0:T(8,128)S(1)}, f32[6,8,128]{2,1,0:T(8,128)}, u32[]{:S(2)}) copy-start(f32[6,8,128]{2,1,0:T(8,128)} %param.7) | copy-start | bytes 73732
  37.3 16.8 %all-to-all-start.2 = ((f32[8,2,8]{2,1,0:T(2,128)}), f32[8,2,8]{2,1,0:T(2,128)S(1)}, u32[]{:S(2)}, u32[]{:S(2)}) async-start(f32[8,2,8]{2,1,0:T(2,128)} %bitcast.15), calls=%async_computation.2 | async-start | bytes 16384 | tf_op jit(solution)/shard_map/all_to_all | solution.py:76
  55.9 0.7 copy-start.20
  55.9 0.7 copy-start.21
  55.9 0.7 copy-start.5
  55.9 0.7 copy-start.4
  55.9 0.8 copy-start.3
  61.3 32.9 %collective-permute-start.3 = (f32[6,32,128]{2,1,0:T(8,128)S(1)}, f32[6,32,128]{2,1,0:T(8,128)}, u32[]{:S(2)}, u32[]{:S(2)}) collective-permute-start(f32[6,32,128]{2,1,0:T(8,128)S(1)} %get-tuple-element.5), channel_id=1, source_target_pairs={{0,4},{4,8},{8,12},{12,16},{16,20},{20,24},{24,28},{1,5},{5,9},{9,... | collective-permute-start | bytes 294920 | tf_op jit(solution)/shard_map/ppermute | solution.py:28
  63.2 31.0 %collective-permute-start.2 = (f32[6,32,128]{2,1,0:T(8,128)S(1)}, f32[6,32,128]{2,1,0:T(8,128)}, u32[]{:S(2)}, u32[]{:S(2)}) collective-permute-start(f32[6,32,128]{2,1,0:T(8,128)S(1)} %get-tuple-element.5), channel_id=1, source_target_pairs={{4,0},{8,4},{12,8},{16,12},{20,16},{24,20},{28,24},{5,1},{9,5},{13... | collective-permute-start | bytes 294920 | tf_op jit(solution)/shard_map/ppermute | solution.py:29
  72.1 11.2 %all-to-all-start.3 = ((f32[8,2,8]{2,1,0:T(2,128)}), f32[8,2,8]{2,1,0:T(2,128)S(1)}, u32[]{:S(2)}, u32[]{:S(2)}) async-start(f32[8,2,8]{2,1,0:T(2,128)} %broadcast_multiply_fusion.3), calls=%async_computation.3 | async-start | bytes 16384 | tf_op jit(solution)/shard_map/all_to_all | solution.py:70
  79.2 4.1 %copy-start.26 = (s32[16]{0:T(128)S(1)}, s32[16]{0:T(128)}, u32[]{:S(2)}) copy-start(s32[16]{0:T(128)} %copy-done.25) | copy-start | bytes 196
  84.4 8.0 %all-to-all-start.4 = ((f32[8,2,8]{2,1,0:T(2,128)}), f32[8,2,8]{2,1,0:T(2,128)S(1)}, u32[]{:S(2)}, u32[]{:S(2)}) async-start(f32[8,2,8]{2,1,0:T(2,128)} %bitcast.25), calls=%async_computation.4 | async-start | bytes 16384 | tf_op jit(solution)/shard_map/all_to_all | solution.py:76
  94.2 0.7 copy-start.16
  94.2 0.7 copy-start.11
  94.2 0.8 copy-start.10
  94.2 0.8 copy-start.9
  99.5 31.7 %collective-permute-start.5 = (f32[6,32,128]{2,1,0:T(8,128)S(1)}, f32[6,32,128]{2,1,0:T(8,128)}, u32[]{:S(2)}, u32[]{:S(2)}) collective-permute-start(f32[6,32,128]{2,1,0:T(8,128)S(1)} %multiply_subtract_fusion.1), channel_id=1, source_target_pairs={{0,4},{4,8},{8,12},{12,16},{16,20},{20,24},{24,28},{1,5},{5,9},{9,... | collective-permute-start | bytes 294920 | tf_op jit(solution)/shard_map/ppermute | solution.py:28
  101.9 29.4 %collective-permute-start.4 = (f32[6,32,128]{2,1,0:T(8,128)S(1)}, f32[6,32,128]{2,1,0:T(8,128)}, u32[]{:S(2)}, u32[]{:S(2)}) collective-permute-start(f32[6,32,128]{2,1,0:T(8,128)S(1)} %multiply_subtract_fusion.1), channel_id=1, source_target_pairs={{4,0},{8,4},{12,8},{16,12},{20,16},{24,20},{28,24},{5,1},{9,5},{13... | collective-permute-start | bytes 294920 | tf_op jit(solution)/shard_map/ppermute | solution.py:29
  110.8 9.4 %all-to-all-start.5 = ((f32[8,2,8]{2,1,0:T(2,128)}), f32[8,2,8]{2,1,0:T(2,128)S(1)}, u32[]{:S(2)}, u32[]{:S(2)}) async-start(f32[8,2,8]{2,1,0:T(2,128)} %broadcast_multiply_fusion.2), calls=%async_computation.5 | async-start | bytes 16384 | tf_op jit(solution)/shard_map/all_to_all | solution.py:70
  116.1 4.1 %copy-start.27 = (s32[16]{0:T(128)S(1)}, s32[16]{0:T(128)}, u32[]{:S(2)}) copy-start(s32[16]{0:T(128)} %copy-done.25) | copy-start | bytes 196
  121.2 8.0 %all-to-all-start.6 = ((f32[8,2,8]{2,1,0:T(2,128)}), f32[8,2,8]{2,1,0:T(2,128)S(1)}, u32[]{:S(2)}, u32[]{:S(2)}) async-start(f32[8,2,8]{2,1,0:T(2,128)} %bitcast.35), calls=%async_computation.6 | async-start | bytes 16384 | tf_op jit(solution)/shard_map/all_to_all | solution.py:76
  131.2 0.7 copy-start.17
  131.2 0.7 copy-start.14
  131.3 0.8 copy-start.13
  131.3 0.8 copy-start.12
  136.6 33.1 %collective-permute-start.7 = (f32[6,32,128]{2,1,0:T(8,128)S(1)}, f32[6,32,128]{2,1,0:T(8,128)}, u32[]{:S(2)}, u32[]{:S(2)}) collective-permute-start(f32[6,32,128]{2,1,0:T(8,128)S(1)} %multiply_subtract_fusion), channel_id=1, source_target_pairs={{0,4},{4,8},{8,12},{12,16},{16,20},{20,24},{24,28},{1,5},{5,9},{9,... | collective-permute-start | bytes 294920 | tf_op jit(solution)/shard_map/ppermute | solution.py:28
  138.9 30.8 %collective-permute-start.6 = (f32[6,32,128]{2,1,0:T(8,128)S(1)}, f32[6,32,128]{2,1,0:T(8,128)}, u32[]{:S(2)}, u32[]{:S(2)}) collective-permute-start(f32[6,32,128]{2,1,0:T(8,128)S(1)} %multiply_subtract_fusion), channel_id=1, source_target_pairs={{4,0},{8,4},{12,8},{16,12},{20,16},{24,20},{28,24},{5,1},{9,5},{13... | collective-permute-start | bytes 294920 | tf_op jit(solution)/shard_map/ppermute | solution.py:29
  147.2 9.4 %all-to-all-start.7 = ((f32[8,2,8]{2,1,0:T(2,128)}), f32[8,2,8]{2,1,0:T(2,128)S(1)}, u32[]{:S(2)}, u32[]{:S(2)}) async-start(f32[8,2,8]{2,1,0:T(2,128)} %broadcast_multiply_fusion.1), calls=%async_computation.7 | async-start | bytes 16384 | tf_op jit(solution)/shard_map/all_to_all | solution.py:70
  152.4 4.1 %copy-start.28 = (s32[16]{0:T(128)S(1)}, s32[16]{0:T(128)}, u32[]{:S(2)}) copy-start(s32[16]{0:T(128)} %copy-done.25) | copy-start | bytes 196
  157.6 8.0 %all-to-all-start.8 = ((f32[8,2,8]{2,1,0:T(2,128)}), f32[8,2,8]{2,1,0:T(2,128)S(1)}, u32[]{:S(2)}, u32[]{:S(2)}) async-start(f32[8,2,8]{2,1,0:T(2,128)} %bitcast.45), calls=%async_computation.8 | async-start | bytes 16384 | tf_op jit(solution)/shard_map/all_to_all | solution.py:76
  168.3 1.4 copy-start.19
  169.7 0.7 copy-start.15
  169.7 0.7 copy-start.8
  169.7 0.8 copy-start.7
  169.7 0.8 copy-start.6
where the time goes:
time: 175 us; the launch traced here: 173 us
  starting transfers between devices  54.7 us (31%)
  local copies, waits for them, and re-layouts  47.6 us (27%)
  waiting for transfers between devices  27.9 us (16%)
  other arithmetic  18.2 us (10%)
  blocking collectives  13.5 us (8%)
  matrix products  10.3 us (6%)
    slice x48, local copies, waits for them, and re-layouts, kinetic(): jnp.roll(grid_field, distance, 1)  21.3 us
    all_to_all x4, starting transfers between devices, owner_side(): lax.all_to_all(partial_value, 'domain', split_axis=0, concat_axis=0, tile...  20.1 us
    all_to_all x4, waiting for transfers between devices, owner_side(): lax.all_to_all(partial_value, 'domain', split_axis=0, concat_axis=0, tile...  15.2 us
    slice x48, local copies, waits for them, and re-layouts, kinetic(): jnp.roll(grid_field, distance, 2)  14.5 us
    all_gather x1, blocking collectives, shards(): pot_full = lax.all_gather(potential, 'band', axis=1, tiled=True)  13.5 us
    all_to_all x4, starting transfers between devices, owner_side(): lax.all_to_all(returned, 'domain', split_axis=0, concat_axis=0, tiled=True)  13.3 us
    all_to_all x4, waiting for transfers between devices, owner_side(): lax.all_to_all(returned, 'domain', split_axis=0, concat_axis=0, tiled=True)  12.7 us
    ppermute x4, starting transfers between devices, extended(): before = lax.ppermute(last, axis, up)  9.69 us
  transfers between devices with their start and end apart: 17, of which 7 were waited for; matrix products, arithmetic and copies ran while one was open for 32% of the time, Pallas kernels for 0%

commit v1 on v0

--- a/solution.py
+++ b/solution.py
@@ -16,6 +16,26 @@
 filter_center = 6.0
 filter_half_width = 4.0
 highest = lax.Precision.HIGHEST
+
+
+def _settle_rows(tile_in):
+    main, p_next = (lax.axis_size("domain"), lax.axis_index("domain"))
+    aux = list(tile_in.shape)
+    front = tile_in.shape[0] // main
+    aux[0] = front
+    z_new = aux[0]
+    aux[0] = z_new * main
+    nth = 0
+    q_next = jnp.zeros(aux, tile_in.dtype)
+    while nth < main:
+        u_next = lax.dynamic_slice_in_dim(tile_in, (p_next ^ nth) * front, front, axis=0)
+        if nth:
+            u_next = lax.ppermute(
+                u_next, axis_name="domain", perm=[(dev, dev ^ nth) for dev in range(main)]
+            )
+        q_next = lax.dynamic_update_slice_in_dim(q_next, u_next, (p_next ^ nth) * z_new, axis=0)
+        nth += 1
+    return q_next
 
 
 def extended(value, sides, width):
@@ -61,7 +81,7 @@
     slot_atoms = intersection[0]
     live_slots = (slot_atoms >= 0).astype(jnp.float32)
     atom_count = dmat.shape[0]
-    incoming = lax.all_to_all(slot_atoms, "domain", split_axis=0, concat_axis=0, tiled=True)
+    incoming = _settle_rows(slot_atoms)
     in_hot = (incoming.reshape(-1)[:, None] == jnp.arange(atom_count, dtype=jnp.int32)).astype(
         jnp.float32
     )

time: 175 us -> 184 us (1.051)
  starting transfers between devices: 54.7 us -> 59.7 us
  waiting for transfers between devices: 27.9 us -> 32.4 us
  local copies, waits for them, and re-layouts: 47.6 us -> 45.6 us
    ppermute x0 -> x7, starting transfers between devices: none -> 11.1 us  [_settle_rows(): lax.ppermute(u_next, axis_name='domain', perm=[(dev, dev ^ nth) for dev i...]
    ppermute x0 -> x7, waiting for transfers between devices: none -> 8 us  [_settle_rows(): lax.ppermute(u_next, axis_name='domain', perm=[(dev, dev ^ nth) for dev i...]
    all_to_all x1 -> x0, starting transfers between devices: 6.47 us -> none  [shards(): lax.all_to_all(slot_atoms, 'domain', split_axis=0, concat_axis=0, tiled=T...]
    all_to_all x4, waiting for transfers between devices: 15.2 us -> 12.3 us  [owner_side(): lax.all_to_all(partial_value, 'domain', split_axis=0, concat_axis=0, tile...]
    all_to_all x2 -> x0, local copies, waits for them, and re-layouts: 1.84 us -> none  [shards(): lax.all_to_all(slot_atoms, 'domain', split_axis=0, concat_axis=0, tiled=T...]
    unnamed x58 -> x65, local copies, waits for them, and re-layouts: 4.31 us -> 3.92 us
  transfers between devices with their start and end apart: 17 -> 23, of which waited for: 7 -> 10; matrix products, arithmetic and copies ran while one was open for 32% -> 30% of each run, Pallas kernels for 0% -> 0%
where the time goes in v1:
time: 184 us; the launch traced here: 182 us
  starting transfers between devices  59.7 us (32%)
  local copies, waits for them, and re-layouts  45.6 us (25%)
  waiting for transfers between devices  32.4 us (18%)
  other arithmetic  17.7 us (10%)
  blocking collectives  13.5 us (7%)
  matrix products  12.1 us (7%)
    slice x48, local copies, waits for them, and re-layouts, kinetic(): jnp.roll(grid_field, distance, 1)  20.9 us
    all_to_all x4, starting transfers between devices, owner_side(): lax.all_to_all(partial_value, 'domain', split_axis=0, concat_axis=0, tile...  20.1 us
    slice x48, local copies, waits for them, and re-layouts, kinetic(): jnp.roll(grid_field, distance, 2)  14.4 us
    all_to_all x4, starting transfers between devices, owner_side(): lax.all_to_all(returned, 'domain', split_axis=0, concat_axis=0, tiled=True)  14.3 us
    all_gather x1, blocking collectives, shards(): pot_full = lax.all_gather(potential, 'band', axis=1, tiled=True)  13.5 us
    all_to_all x4, waiting for transfers between devices, owner_side(): lax.all_to_all(partial_value, 'domain', split_axis=0, concat_axis=0, tile...  12.3 us
    all_to_all x4, waiting for transfers between devices, owner_side(): lax.all_to_all(returned, 'domain', split_axis=0, concat_axis=0, tiled=True)  12.1 us
    ppermute x7, starting transfers between devices, _settle_rows(): lax.ppermute(u_next, axis_name='domain', perm=[(dev, dev ^ nth) for dev i...  11.1 us
  transfers between devices with their start and end apart: 23, of which 10 were waited for; matrix products, arithmetic and copies ran while one was open for 30% of the time, Pallas kernels for 0%

profile of v1, /device:TPU:0, one launch (start us, length us, event | category | flops | bytes accessed | tf_op | source)
XLA Modules:
  0.0 182.1 jit_solution(5039480277541216095)
XLA Ops:
  0.0 2.5 %collective-permute-start.1 = (f32[6,32,128]{2,1,0:T(8,128)}, f32[6,32,128]{2,1,0:T(8,128)S(1)}, u32[]{:S(2)}, u32[]{:S(2)}) collective-permute-start(f32[6,32,128]{2,1,0:T(8,128)} %bitcast.131), channel_id=1, source_target_pairs={{0,4},{4,8},{8,12},{12,16},{16,20},{20,24},{24,28},{1,5},{5,9},{9,... | collective-permute-start | bytes 294920 | tf_op jit(solution)/shard_map/ppermute | solution.py:48
  2.5 1.3 collective-permute-start
  3.8 1.3 fusion.256
  5.1 5.9 %collective-permute-start.7 = (s32[1,2]{1,0:T(1,128)S(1)}, s32[1,2]{1,0:T(1,128)S(1)}, u32[]{:S(2)}, u32[]{:S(2)}) collective-permute-start(s32[1,2]{1,0:T(1,128)S(1)} %bitcast.196), channel_id=1, source_target_pairs={{0,24},{4,28},{8,16},{12,20},{16,8},{20,12},{24,0},{28,4},{1,25},{... | collective-permute-start | bytes 32 | tf_op jit(solution)/shard_map/ppermute | solution.py:33
  13.6 1.1 fusion.14
  15.3 4.1 %all-to-all-start = ((f32[8,2,8]{2,1,0:T(2,128)}), f32[8,2,8]{2,1,0:T(2,128)S(1)}, u32[]{:S(2)}, u32[]{:S(2)}) async-start(f32[8,2,8]{2,1,0:T(2,128)} %broadcast_multiply_fusion.4), calls=%async_computation | async-start | bytes 16384 | tf_op jit(solution)/shard_map/all_to_all | solution.py:90
  23.9 0.7 fusion.334
  24.7 0.7 fusion.333
  26.8 0.7 fusion.353
  27.5 0.7 fusion.354
  28.5 2.1 %collective-permute-start.3 = (s32[1,2]{1,0:T(1,128)S(1)}, s32[1,2]{1,0:T(1,128)S(1)}, u32[]{:S(2)}, u32[]{:S(2)}) collective-permute-start(s32[1,2]{1,0:T(1,128)S(1)} %bitcast.200), channel_id=1, source_target_pairs={{0,8},{4,12},{8,0},{12,4},{16,24},{20,28},{24,16},{28,20},{1,9},{5... | collective-permute-start | bytes 32 | tf_op jit(solution)/shard_map/ppermute | solution.py:33
  30.6 1.5 collective-permute-done.3
  32.7 2.3 %collective-permute-done.4 = s32[1,2]{1,0:T(1,128)S(1)} collective-permute-done((s32[1,2]{1,0:T(1,128)S(1)}, s32[1,2]{1,0:T(1,128)S(1)}, u32[]{:S(2)}, u32[]{:S(2)}) %collective-permute-start.4) | collective-permute-done | bytes 40 | tf_op jit(solution)/shard_map/ppermute | solution.py:33
  35.0 2.0 %collective-permute-start.5 = (s32[1,2]{1,0:T(1,128)S(1)}, s32[1,2]{1,0:T(1,128)S(1)}, u32[]{:S(2)}, u32[]{:S(2)}) collective-permute-start(s32[1,2]{1,0:T(1,128)S(1)} %bitcast.198), channel_id=1, source_target_pairs={{0,16},{4,20},{8,24},{12,28},{16,0},{20,4},{24,8},{28,12},{1,17},{... | collective-permute-start | bytes 32 | tf_op jit(solution)/shard_map/ppermute | solution.py:33
  37.1 1.5 collective-permute-done.5
  38.9 2.7 %collective-permute-done.6 = s32[1,2]{1,0:T(1,128)S(1)} collective-permute-done((s32[1,2]{1,0:T(1,128)S(1)}, s32[1,2]{1,0:T(1,128)S(1)}, u32[]{:S(2)}, u32[]{:S(2)}) %collective-permute-start.6) | collective-permute-done | bytes 40 | tf_op jit(solution)/shard_map/ppermute | solution.py:33
  42.4 0.8 fusion.238
  43.2 4.2 %all-to-all-start.1 = ((f32[8,2,8]{2,1,0:T(2,128)}), f32[8,2,8]{2,1,0:T(2,128)S(1)}, u32[]{:S(2)}, u32[]{:S(2)}) async-start(f32[8,2,8]{2,1,0:T(2,128)} %bitcast.14), calls=%async_computation.1 | async-start | bytes 16384 | tf_op jit(solution)/shard_map/all_to_all | solution.py:96
  47.4 13.5 %all_gather.3 = f32[6,32,128]{2,1,0:T(8,128)S(1)} all-gather(f32[6,8,128]{2,1,0:T(8,128)S(1)} %copy-done.20), channel_id=1, replica_groups=mesh['domain'=8,'band'=4] {'band'}, dimensions={1}, use_global_device_ids=true | all-gather | bytes 122880 | tf_op jit(solution)/shard_map/all_gather | solution.py:74
  62.1 1.3 scatter_custom_fusion
  64.3 2.1 %broadcast_multiply_fusion = (f32[6,32,128]{2,1,0:T(8,128)S(1)}, f32[6,32,128]{2,1,0:T(8,128)S(1)}) fusion(f32[6,32,128]{2,1,0:T(8,128)S(1)} %bitcast.158, f32[6,32,128]{2,1,0:T(8,128)S(1)} %bitcast.162, f32[6,32,128]{2,1,0:T(8,128)S(1)} %all_gather.3, f32[6,32,6]{2,1,0:T(8,128)} %get-tuple-element.204, f32[6,32,122]{2,1,0:T(8,128)} %get-tuple-element.206, ...), kind=kLoop, calls=%fused_computation.315 | loop fusion | flops 2064384 | bytes 3047424 | tf_op jit(solution)/shard_map/div | solution.py:115
  68.9 1.9 %collective-permute-start.10 = (f32[6,32,128]{2,1,0:T(8,128)S(1)}, f32[6,32,128]{2,1,0:T(8,128)}, u32[]{:S(2)}, u32[]{:S(2)}) collective-permute-start(f32[6,32,128]{2,1,0:T(8,128)S(1)} %get-tuple-element.13), channel_id=1, source_target_pairs={{0,4},{4,8},{8,12},{12,16},{16,20},{20,24},{24,28},{1,5},{5,9},{9,... | collective-permute-start | bytes 294920 | tf_op jit(solution)/shard_map/ppermute | solution.py:48
  70.8 1.3 collective-permute-start.9
  74.3 0.7 fusion.325
  75.0 0.7 fusion.310
  77.8 0.8 gather_fusion.1
  78.6 1.1 fusion.10
  80.3 6.6 %all-to-all-start.2 = ((f32[8,2,8]{2,1,0:T(2,128)}), f32[8,2,8]{2,1,0:T(2,128)S(1)}, u32[]{:S(2)}, u32[]{:S(2)}) async-start(f32[8,2,8]{2,1,0:T(2,128)} %broadcast_multiply_fusion.3), calls=%async_computation.2 | async-start | bytes 16384 | tf_op jit(solution)/shard_map/all_to_all | solution.py:90
  87.6 4.1 %all-to-all-done.2 = f32[8,2,8]{2,1,0:T(2,128)S(1)} async-done(((f32[8,2,8]{2,1,0:T(2,128)}), f32[8,2,8]{2,1,0:T(2,128)S(1)}, u32[]{:S(2)}, u32[]{:S(2)}) %all-to-all-start.2) | async-done | bytes 544 | tf_op jit(solution)/shard_map/all_to_all | solution.py:90
  92.3 0.8 fusion.236
  93.1 3.3 %all-to-all-start.3 = ((f32[8,2,8]{2,1,0:T(2,128)}), f32[8,2,8]{2,1,0:T(2,128)S(1)}, u32[]{:S(2)}, u32[]{:S(2)}) async-start(f32[8,2,8]{2,1,0:T(2,128)} %bitcast.28), calls=%async_computation.3 | async-start | bytes 16384 | tf_op jit(solution)/shard_map/all_to_all | solution.py:96
  97.1 4.0 %all-to-all-done.3 = f32[8,2,8]{2,1,0:T(2,128)S(1)} async-done(((f32[8,2,8]{2,1,0:T(2,128)}), f32[8,2,8]{2,1,0:T(2,128)S(1)}, u32[]{:S(2)}, u32[]{:S(2)}) %all-to-all-start.3) | async-done | bytes 544 | tf_op jit(solution)/shard_map/all_to_all | solution.py:96
  101.8 1.2 scatter_custom_fusion.1
  103.8 2.2 %multiply_subtract_fusion.1 = f32[6,32,128]{2,1,0:T(8,128)S(1)} fusion(f32[6,32,128]{2,1,0:T(8,128)S(1)} %get-tuple-element.14, f32[6,32,128]{2,1,0:T(8,128)S(1)} %bitcast.163, f32[6,32,128]{2,1,0:T(8,128)S(1)} %all_gather.3, f32[6,32,128]{2,1,0:T(8,128)S(1)} %get-tuple-element.13, f32[6,32,6]{2,1,0:T(8,128)S(1)} %get-tuple-element.156, ...), kind=kLoop, calls=%fused_computation.310 | loop fusion | flops 2088960 | bytes 3145728 | tf_op jit(solution)/shard_map/sub | solution.py:118
  108.4 2.3 %collective-permute-start.12 = (f32[6,32,128]{2,1,0:T(8,128)S(1)}, f32[6,32,128]{2,1,0:T(8,128)}, u32[]{:S(2)}, u32[]{:S(2)}) collective-permute-start(f32[6,32,128]{2,1,0:T(8,128)S(1)} %multiply_subtract_fusion.1), channel_id=1, source_target_pairs={{0,4},{4,8},{8,12},{12,16},{16,20},{20,24},{24,28},{1,5},{5,9},{9,... | collective-permute-start | bytes 294920 | tf_op jit(solution)/shard_map/ppermute | solution.py:48
  110.7 1.3 collective-permute-start.11
  112.9 0.7 fusion.302
  113.6 0.7 fusion.301
  114.3 0.7 fusion.286
  115.0 0.7 fusion.285
  117.2 0.8 gather_fusion.2
  117.9 1.1 fusion.6
  119.7 4.7 %all-to-all-start.4 = ((f32[8,2,8]{2,1,0:T(2,128)}), f32[8,2,8]{2,1,0:T(2,128)S(1)}, u32[]{:S(2)}, u32[]{:S(2)}) async-start(f32[8,2,8]{2,1,0:T(2,128)} %broadcast_multiply_fusion.2), calls=%async_computation.4 | async-start | bytes 16384 | tf_op jit(solution)/shard_map/all_to_all | solution.py:90
  124.9 4.1 %all-to-all-done.4 = f32[8,2,8]{2,1,0:T(2,128)S(1)} async-done(((f32[8,2,8]{2,1,0:T(2,128)}), f32[8,2,8]{2,1,0:T(2,128)S(1)}, u32[]{:S(2)}, u32[]{:S(2)}) %all-to-all-start.4) | async-done | bytes 544 | tf_op jit(solution)/shard_map/all_to_all | solution.py:90
  129.7 0.8 fusion.234
  130.5 3.5 %all-to-all-start.5 = ((f32[8,2,8]{2,1,0:T(2,128)}), f32[8,2,8]{2,1,0:T(2,128)S(1)}, u32[]{:S(2)}, u32[]{:S(2)}) async-start(f32[8,2,8]{2,1,0:T(2,128)} %bitcast.42), calls=%async_computation.5 | async-start | bytes 16384 | tf_op jit(solution)/shard_map/all_to_all | solution.py:96
  134.6 4.0 %all-to-all-done.5 = f32[8,2,8]{2,1,0:T(2,128)S(1)} async-done(((f32[8,2,8]{2,1,0:T(2,128)}), f32[8,2,8]{2,1,0:T(2,128)S(1)}, u32[]{:S(2)}, u32[]{:S(2)}) %all-to-all-start.5) | async-done | bytes 544 | tf_op jit(solution)/shard_map/all_to_all | solution.py:96
  139.3 1.2 scatter_custom_fusion.2
  141.3 2.2 %multiply_subtract_fusion = f32[6,32,128]{2,1,0:T(8,128)S(1)} fusion(f32[6,32,128]{2,1,0:T(8,128)S(1)} %multiply_subtract_fusion.1, f32[6,32,128]{2,1,0:T(8,128)S(1)} %bitcast.164, f32[6,32,128]{2,1,0:T(8,128)S(1)} %all_gather.3, f32[6,32,6]{2,1,0:T(8,128)S(1)} %get-tuple-element.108, f32[6,32,122]{2,1,0:T(8,128)S(1)} %get-tuple-element.110, ...), kind=kLoop, calls=%fused_computation.309 | loop fusion | flops 2113536 | bytes 3047424 | tf_op jit(solution)/shard_map/sub | solution.py:118
  145.9 2.3 %collective-permute-start.14 = (f32[6,32,128]{2,1,0:T(8,128)S(1)}, f32[6,32,128]{2,1,0:T(8,128)}, u32[]{:S(2)}, u32[]{:S(2)}) collective-permute-start(f32[6,32,128]{2,1,0:T(8,128)S(1)} %multiply_subtract_fusion), channel_id=1, source_target_pairs={{0,4},{4,8},{8,12},{12,16},{16,20},{20,24},{24,28},{1,5},{5,9},{9,... | collective-permute-start | bytes 294920 | tf_op jit(solution)/shard_map/ppermute | solution.py:48
  148.2 1.3 collective-permute-start.13
  151.0 0.7 fusion.262
  151.7 0.7 fusion.261
  152.4 0.7 fusion.281
  153.9 0.7 fusion.282
  154.6 0.8 gather_fusion.3
  155.4 1.1 fusion.2
  157.1 4.7 %all-to-all-start.6 = ((f32[8,2,8]{2,1,0:T(2,128)}), f32[8,2,8]{2,1,0:T(2,128)S(1)}, u32[]{:S(2)}, u32[]{:S(2)}) async-start(f32[8,2,8]{2,1,0:T(2,128)} %broadcast_multiply_fusion.1), calls=%async_computation.6 | async-start | bytes 16384 | tf_op jit(solution)/shard_map/all_to_all | solution.py:90
  162.4 4.1 %all-to-all-done.6 = f32[8,2,8]{2,1,0:T(2,128)S(1)} async-done(((f32[8,2,8]{2,1,0:T(2,128)}), f32[8,2,8]{2,1,0:T(2,128)S(1)}, u32[]{:S(2)}, u32[]{:S(2)}) %all-to-all-start.6) | async-done | bytes 544 | tf_op jit(solution)/shard_map/all_to_all | solution.py:90
  167.1 0.8 fusion.232
  167.9 3.3 %all-to-all-start.7 = ((f32[8,2,8]{2,1,0:T(2,128)}), f32[8,2,8]{2,1,0:T(2,128)S(1)}, u32[]{:S(2)}, u32[]{:S(2)}) async-start(f32[8,2,8]{2,1,0:T(2,128)} %bitcast.56), calls=%async_computation.7 | async-start | bytes 16384 | tf_op jit(solution)/shard_map/all_to_all | solution.py:96
  171.8 4.0 %all-to-all-done.7 = f32[8,2,8]{2,1,0:T(2,128)S(1)} async-done(((f32[8,2,8]{2,1,0:T(2,128)}), f32[8,2,8]{2,1,0:T(2,128)S(1)}, u32[]{:S(2)}, u32[]{:S(2)}) %all-to-all-start.7) | async-done | bytes 544 | tf_op jit(solution)/shard_map/all_to_all | solution.py:96
  177.2 1.4 scatter_custom_fusion.3
  179.4 2.7 %subtract_bitcast_fusion = f32[1,6,32,128]{3,2,1,0:T(8,128)} fusion(f32[6,32,128]{2,1,0:T(8,128)S(1)} %multiply_subtract_fusion.1, f32[6,32,128]{2,1,0:T(8,128)S(1)} %multiply_subtract_fusion, f32[6,32,128]{2,1,0:T(8,128)S(1)} %bitcast.161, f32[6,32,128]{2,1,0:T(8,128)S(1)} %all_gather.3, f32[6,32,6]{2,1,0:T(8,128)} %get-tuple-element.60, ...), kind=kLoop, calls=%fused_computation.308 | loop fusion | flops 2088960 | bytes 3047424 | tf_op jit(solution)/shard_map/broadcast_in_dim | solution.py:121
  (206 shorter events, 41.2 us)
Async XLA Ops:
  0.0 13.6 %copy-start = (f32[1,8,2,8,1024]{4,3,2,1,0:T(8,128)S(1)}, f32[1,8,2,8,1024]{4,3,2,1,0:T(8,128)}, u32[]{:S(2)}) copy-start(f32[1,8,2,8,1024]{4,3,2,1,0:T(8,128)} %param.8) | copy-start | bytes 1572868
  0.0 12.9 %copy-start.1 = (f32[1,6,32,128]{3,2,1,0:T(8,128)S(1)}, f32[1,6,32,128]{3,2,1,0:T(8,128)}, u32[]{:S(2)}) copy-start(f32[1,6,32,128]{3,2,1,0:T(8,128)} %param.6) | copy-start | bytes 294916
  0.0 63.5 %collective-permute-start.1 = (f32[6,32,128]{2,1,0:T(8,128)}, f32[6,32,128]{2,1,0:T(8,128)S(1)}, u32[]{:S(2)}, u32[]{:S(2)}) collective-permute-start(f32[6,32,128]{2,1,0:T(8,128)} %bitcast.131), channel_id=1, source_target_pairs={{0,4},{4,8},{8,12},{12,16},{16,20},{20,24},{24,28},{1,5},{5,9},{9,... | collective-permute-start | bytes 294920 | tf_op jit(solution)/shard_map/ppermute | solution.py:48
  2.5 61.0 %collective-permute-start = (f32[6,32,128]{2,1,0:T(8,128)}, f32[6,32,128]{2,1,0:T(8,128)}, u32[]{:S(2)}, u32[]{:S(2)}) collective-permute-start(f32[6,32,128]{2,1,0:T(8,128)} %bitcast.132), channel_id=1, source_target_pairs={{4,0},{8,4},{12,8},{16,12},{20,16},{24,20},{28,24},{5,1},{9,5},{13... | collective-permute-start | bytes 294920 | tf_op jit(solution)/shard_map/ppermute | solution.py:49
  5.1 36.5 %collective-permute-start.7 = (s32[1,2]{1,0:T(1,128)S(1)}, s32[1,2]{1,0:T(1,128)S(1)}, u32[]{:S(2)}, u32[]{:S(2)}) collective-permute-start(s32[1,2]{1,0:T(1,128)S(1)} %bitcast.196), channel_id=1, source_target_pairs={{0,24},{4,28},{8,16},{12,20},{16,8},{20,12},{24,0},{28,4},{1,25},{... | collective-permute-start | bytes 32 | tf_op jit(solution)/shard_map/ppermute | solution.py:33
  11.0 30.6 %collective-permute-start.8 = (s32[1,2]{1,0:T(1,128)S(1)}, s32[1,2]{1,0:T(1,128)S(1)}, u32[]{:S(2)}, u32[]{:S(2)}) collective-permute-start(s32[1,2]{1,0:T(1,128)S(1)} %bitcast.195), channel_id=1, source_target_pairs={{0,28},{4,24},{8,20},{12,16},{16,12},{20,8},{24,4},{28,0},{1,29},{... | collective-permute-start | bytes 32 | tf_op jit(solution)/shard_map/ppermute | solution.py:33
  11.0 17.5 %collective-permute-start.2 = (s32[1,2]{1,0:T(1,128)S(1)}, s32[1,2]{1,0:T(1,128)S(1)}, u32[]{:S(2)}, u32[]{:S(2)}) collective-permute-start(s32[1,2]{1,0:T(1,128)S(1)} %bitcast.201), channel_id=1, source_target_pairs={{0,4},{4,0},{8,12},{12,8},{16,20},{20,16},{24,28},{28,24},{1,5},{5... | collective-permute-start | bytes 32 | tf_op jit(solution)/shard_map/ppermute | solution.py:33
  11.9 0.7 copy-start.26
  12.9 49.2 %copy-start.27 = (s32[128]{0:T(128)}, s32[128]{0:T(128)S(1)}, u32[]{:S(2)}) copy-start(s32[128]{0:T(128)S(1)} %fusion.257) | copy-start | bytes 1540
  12.9 0.7 copy-start.25
  15.3 26.4 %all-to-all-start = ((f32[8,2,8]{2,1,0:T(2,128)}), f32[8,2,8]{2,1,0:T(2,128)S(1)}, u32[]{:S(2)}, u32[]{:S(2)}) async-start(f32[8,2,8]{2,1,0:T(2,128)} %broadcast_multiply_fusion.4), calls=%async_computation | async-start | bytes 16384 | tf_op jit(solution)/shard_map/all_to_all | solution.py:90
  27.5 0.8 copy-start.19
  28.5 3.6 %collective-permute-start.3 = (s32[1,2]{1,0:T(1,128)S(1)}, s32[1,2]{1,0:T(1,128)S(1)}, u32[]{:S(2)}, u32[]{:S(2)}) collective-permute-start(s32[1,2]{1,0:T(1,128)S(1)} %bitcast.200), channel_id=1, source_target_pairs={{0,8},{4,12},{8,0},{12,4},{16,24},{20,28},{24,16},{28,20},{1,9},{5... | collective-permute-start | bytes 32 | tf_op jit(solution)/shard_map/ppermute | solution.py:33
  32.1 3.0 %collective-permute-start.4 = (s32[1,2]{1,0:T(1,128)S(1)}, s32[1,2]{1,0:T(1,128)S(1)}, u32[]{:S(2)}, u32[]{:S(2)}) collective-permute-start(s32[1,2]{1,0:T(1,128)S(1)} %bitcast.199), channel_id=1, source_target_pairs={{0,12},{4,8},{8,4},{12,0},{16,28},{20,24},{24,20},{28,16},{1,13},{... | collective-permute-start | bytes 32 | tf_op jit(solution)/shard_map/ppermute | solution.py:33
  35.0 3.6 %collective-permute-start.5 = (s32[1,2]{1,0:T(1,128)S(1)}, s32[1,2]{1,0:T(1,128)S(1)}, u32[]{:S(2)}, u32[]{:S(2)}) collective-permute-start(s32[1,2]{1,0:T(1,128)S(1)} %bitcast.198), channel_id=1, source_target_pairs={{0,16},{4,20},{8,24},{12,28},{16,0},{20,4},{24,8},{28,12},{1,17},{... | collective-permute-start | bytes 32 | tf_op jit(solution)/shard_map/ppermute | solution.py:33
  38.6 3.0 %collective-permute-start.6 = (s32[1,2]{1,0:T(1,128)S(1)}, s32[1,2]{1,0:T(1,128)S(1)}, u32[]{:S(2)}, u32[]{:S(2)}) collective-permute-start(s32[1,2]{1,0:T(1,128)S(1)} %bitcast.197), channel_id=1, source_target_pairs={{0,20},{4,16},{8,28},{12,24},{16,4},{20,0},{24,12},{28,8},{1,21},{... | collective-permute-start | bytes 32 | tf_op jit(solution)/shard_map/ppermute | solution.py:33
  41.8 0.6 copy-start.28
  42.4 5.0 %copy-start.20 = (f32[6,8,128]{2,1,0:T(8,128)S(1)}, f32[6,8,128]{2,1,0:T(8,128)}, u32[]{:S(2)}) copy-start(f32[6,8,128]{2,1,0:T(8,128)} %param.7) | copy-start | bytes 73732
  43.2 17.6 %all-to-all-start.1 = ((f32[8,2,8]{2,1,0:T(2,128)}), f32[8,2,8]{2,1,0:T(2,128)S(1)}, u32[]{:S(2)}, u32[]{:S(2)}) async-start(f32[8,2,8]{2,1,0:T(2,128)} %bitcast.14), calls=%async_computation.1 | async-start | bytes 16384 | tf_op jit(solution)/shard_map/all_to_all | solution.py:96
  63.5 0.6 copy-start.15
  63.5 0.8 copy-start.5
  63.5 0.8 copy-start.4
  63.5 0.8 copy-start.3
  68.9 34.0 %collective-permute-start.10 = (f32[6,32,128]{2,1,0:T(8,128)S(1)}, f32[6,32,128]{2,1,0:T(8,128)}, u32[]{:S(2)}, u32[]{:S(2)}) collective-permute-start(f32[6,32,128]{2,1,0:T(8,128)S(1)} %get-tuple-element.13), channel_id=1, source_target_pairs={{0,4},{4,8},{8,12},{12,16},{16,20},{20,24},{24,28},{1,5},{5,9},{9,... | collective-permute-start | bytes 294920 | tf_op jit(solution)/shard_map/ppermute | solution.py:48
  70.8 32.1 %collective-permute-start.9 = (f32[6,32,128]{2,1,0:T(8,128)S(1)}, f32[6,32,128]{2,1,0:T(8,128)}, u32[]{:S(2)}, u32[]{:S(2)}) collective-permute-start(f32[6,32,128]{2,1,0:T(8,128)S(1)} %get-tuple-element.13), channel_id=1, source_target_pairs={{4,0},{8,4},{12,8},{16,12},{20,16},{24,20},{28,24},{5,1},{9,5},{13... | collective-permute-start | bytes 294920 | tf_op jit(solution)/shard_map/ppermute | solution.py:49
  80.3 11.4 %all-to-all-start.2 = ((f32[8,2,8]{2,1,0:T(2,128)}), f32[8,2,8]{2,1,0:T(2,128)S(1)}, u32[]{:S(2)}, u32[]{:S(2)}) async-start(f32[8,2,8]{2,1,0:T(2,128)} %broadcast_multiply_fusion.3), calls=%async_computation.2 | async-start | bytes 16384 | tf_op jit(solution)/shard_map/all_to_all | solution.py:90
  87.6 4.1 %copy-start.29 = (s32[16]{0:T(128)S(1)}, s32[16]{0:T(128)}, u32[]{:S(2)}) copy-start(s32[16]{0:T(128)} %copy-done.28) | copy-start | bytes 196
  93.1 8.0 %all-to-all-start.3 = ((f32[8,2,8]{2,1,0:T(2,128)}), f32[8,2,8]{2,1,0:T(2,128)S(1)}, u32[]{:S(2)}, u32[]{:S(2)}) async-start(f32[8,2,8]{2,1,0:T(2,128)} %bitcast.28), calls=%async_computation.3 | async-start | bytes 16384 | tf_op jit(solution)/shard_map/all_to_all | solution.py:96
  103.0 0.7 copy-start.17
  103.0 0.7 copy-start.22
  103.0 0.8 copy-start.11
  103.0 0.8 copy-start.10
  103.0 0.8 copy-start.9
  108.4 32.1 %collective-permute-start.12 = (f32[6,32,128]{2,1,0:T(8,128)S(1)}, f32[6,32,128]{2,1,0:T(8,128)}, u32[]{:S(2)}, u32[]{:S(2)}) collective-permute-start(f32[6,32,128]{2,1,0:T(8,128)S(1)} %multiply_subtract_fusion.1), channel_id=1, source_target_pairs={{0,4},{4,8},{8,12},{12,16},{16,20},{20,24},{24,28},{1,5},{5,9},{9,... | collective-permute-start | bytes 294920 | tf_op jit(solution)/shard_map/ppermute | solution.py:48
  110.7 29.7 %collective-permute-start.11 = (f32[6,32,128]{2,1,0:T(8,128)S(1)}, f32[6,32,128]{2,1,0:T(8,128)}, u32[]{:S(2)}, u32[]{:S(2)}) collective-permute-start(f32[6,32,128]{2,1,0:T(8,128)S(1)} %multiply_subtract_fusion.1), channel_id=1, source_target_pairs={{4,0},{8,4},{12,8},{16,12},{20,16},{24,20},{28,24},{5,1},{9,5},{13... | collective-permute-start | bytes 294920 | tf_op jit(solution)/shard_map/ppermute | solution.py:49
  119.7 9.4 %all-to-all-start.4 = ((f32[8,2,8]{2,1,0:T(2,128)}), f32[8,2,8]{2,1,0:T(2,128)S(1)}, u32[]{:S(2)}, u32[]{:S(2)}) async-start(f32[8,2,8]{2,1,0:T(2,128)} %broadcast_multiply_fusion.2), calls=%async_computation.4 | async-start | bytes 16384 | tf_op jit(solution)/shard_map/all_to_all | solution.py:90
  124.9 4.1 %copy-start.30 = (s32[16]{0:T(128)S(1)}, s32[16]{0:T(128)}, u32[]{:S(2)}) copy-start(s32[16]{0:T(128)} %copy-done.28) | copy-start | bytes 196
  130.5 8.2 %all-to-all-start.5 = ((f32[8,2,8]{2,1,0:T(2,128)}), f32[8,2,8]{2,1,0:T(2,128)S(1)}, u32[]{:S(2)}, u32[]{:S(2)}) async-start(f32[8,2,8]{2,1,0:T(2,128)} %bitcast.42), calls=%async_computation.5 | async-start | bytes 16384 | tf_op jit(solution)/shard_map/all_to_all | solution.py:96
  140.5 0.7 copy-start.18
  140.5 0.7 copy-start.23
  140.5 0.8 copy-start.14
  140.5 0.8 copy-start.13
  140.5 0.8 copy-start.12
  145.9 32.7 %collective-permute-start.14 = (f32[6,32,128]{2,1,0:T(8,128)S(1)}, f32[6,32,128]{2,1,0:T(8,128)}, u32[]{:S(2)}, u32[]{:S(2)}) collective-permute-start(f32[6,32,128]{2,1,0:T(8,128)S(1)} %multiply_subtract_fusion), channel_id=1, source_target_pairs={{0,4},{4,8},{8,12},{12,16},{16,20},{20,24},{24,28},{1,5},{5,9},{9,... | collective-permute-start | bytes 294920 | tf_op jit(solution)/shard_map/ppermute | solution.py:48
  148.2 30.3 %collective-permute-start.13 = (f32[6,32,128]{2,1,0:T(8,128)S(1)}, f32[6,32,128]{2,1,0:T(8,128)}, u32[]{:S(2)}, u32[]{:S(2)}) collective-permute-start(f32[6,32,128]{2,1,0:T(8,128)S(1)} %multiply_subtract_fusion), channel_id=1, source_target_pairs={{4,0},{8,4},{12,8},{16,12},{20,16},{24,20},{28,24},{5,1},{9,5},{13... | collective-permute-start | bytes 294920 | tf_op jit(solution)/shard_map/ppermute | solution.py:49
  157.1 9.4 %all-to-all-start.6 = ((f32[8,2,8]{2,1,0:T(2,128)}), f32[8,2,8]{2,1,0:T(2,128)S(1)}, u32[]{:S(2)}, u32[]{:S(2)}) async-start(f32[8,2,8]{2,1,0:T(2,128)} %broadcast_multiply_fusion.1), calls=%async_computation.6 | async-start | bytes 16384 | tf_op jit(solution)/shard_map/all_to_all | solution.py:90
  162.4 4.1 %copy-start.31 = (s32[16]{0:T(128)S(1)}, s32[16]{0:T(128)}, u32[]{:S(2)}) copy-start(s32[16]{0:T(128)} %copy-done.28) | copy-start | bytes 196
  167.9 8.0 %all-to-all-start.7 = ((f32[8,2,8]{2,1,0:T(2,128)}), f32[8,2,8]{2,1,0:T(2,128)S(1)}, u32[]{:S(2)}, u32[]{:S(2)}) async-start(f32[8,2,8]{2,1,0:T(2,128)} %bitcast.56), calls=%async_computation.7 | async-start | bytes 16384 | tf_op jit(solution)/shard_map/all_to_all | solution.py:96
  177.1 1.5 copy-start.2
  177.2 1.5 copy-start.24
  178.6 0.7 copy-start.16
  178.6 0.7 copy-start.21
  178.6 0.8 copy-start.8
  178.6 0.8 copy-start.7
  178.6 0.8 copy-start.6
